TPU v7x, 32 devices: a whole 2x2x4 slice. The times are simulated.
32 devices in a mesh: dp: 8 (over y, x, core), seq: 4 (over z).
Axes of the slice: x: 2, y: 2, z: 4, core: 2. Of those that a mesh axis runs over, the one named last changes fastest.
Arguments:
- block_input: bfloat16 [2, 8, 1024, 768], P(None, 'dp', 'seq'), may hold values from -6 to 6
- cotangent: bfloat16 [2, 8, 1024, 768], P(None, 'dp', 'seq'), may hold values from -6 to 6
- segments: int32 [2, 8, 1024], P(None, 'dp'), may hold values from 0 to 3, never falling along the last dimension, each value on 1 to 768 neighbouring positions
- rand_blocks: int32 [12, 16, 3], replicated, may hold values from 0 to 15
- w_attn: float32 [768, 2304], P('dp'), may hold values from -0.21875 to 0.21875
- w_out: float32 [768, 768], P('dp'), may hold values from -1.5 to 1.5
- w_up: float32 [768, 3072], P('dp'), may hold values from -0.21875 to 0.21875
- w_down: float32 [3072, 768], P('dp'), may hold values from -0.109375 to 0.109375
- up_bias: float32 [3072], P('dp'), may hold values from -3 to 3
- bias_rows: float32 [6, 768], P(None, 'dp'), may hold values from -2 to 2
- norm_gains: float32 [2, 768], P(None, 'dp'), may hold values from 0.25 to 1.75
Outputs:
- block_output: bfloat16 [2, 8, 1024, 768], P(None, 'dp', 'seq')
- input_grad: float32 [2, 8, 1024, 768], P(None, 'dp', 'seq')
- grad_w_attn: float32 [768, 2304], P('dp')
- grad_w_out: float32 [768, 768], P('dp')
- grad_w_up: float32 [768, 3072], P('dp')
- grad_w_down: float32 [3072, 768], P('dp')
- grad_up_bias: float32 [3072], P('dp')
- grad_bias_rows: float32 [6, 768], P(None, 'dp')
- grad_norm_gains: float32 [2, 768], P(None, 'dp')
Inputs may be any that keep to these rules, and one draw needn't show every extreme that they name: `segments`: segment numbers never fall along a sequence. `rand_blocks`: block numbers within the sequence.
All inputs are finite; a program needn't handle non-finite values.
Results may differ from a plain program's by a relative error of at most 0.018.
Values may be sent and summed in bfloat16 or wider, within the bound.
No kernel may reach another device: no remote copies, remote signals or barrier semaphores. Data moves between devices by JAX's collectives and lax.ppermute only.
A program may use at most 192 MiB of HBM per device.

v0:
```python
import jax
import jax.numpy as jnp
from jax import lax
from jax.sharding import PartitionSpec as P

EPSILON = 1e-05
MASKED = -1e30


def layer_norm(tensor, gain_row, offset):
    centre = tensor - jnp.mean(tensor, axis=-1, keepdims=True)
    spread = jnp.mean(centre * centre, axis=-1, keepdims=True)
    return centre * lax.rsqrt(spread + EPSILON) * gain_row + offset


def gelu_exact(tensor):
    return jax.nn.gelu(tensor, approximate=False)


def col_sums(tensor):
    return jnp.sum(tensor.astype(jnp.float32), axis=0)


def outer_grad(left, right):
    return lax.dot_general(
        left, right, (((0,), (0,)), ((), ())), preferred_element_type=jnp.float32
    )


def times_transposed(left, right):
    return lax.dot_general(
        left, right, (((1,), (1,)), ((), ())), preferred_element_type=jnp.float32
    )


def cast_half(params):
    return tuple((member.astype(jnp.bfloat16) for member in params))


def visible_mask(rand_blocks, first_row, local_rows, seq_len):
    head_count = rand_blocks.shape[0]
    nblocks = rand_blocks.shape[1]
    block_len = seq_len // nblocks
    local_blocks = local_rows // block_len
    query_block = (first_row + jnp.arange(local_rows, dtype=jnp.int32)) // block_len
    key_block = jnp.arange(seq_len, dtype=jnp.int32) // block_len
    nearby = jnp.abs(query_block[:, None] - key_block[None, :]) <= 1
    global_q = (query_block == 0) | (query_block == nblocks - 1)
    global_k = (key_block == 0) | (key_block == nblocks - 1)
    always = nearby | global_q[:, None] | global_k[None, :]
    chosen = lax.dynamic_slice_in_dim(rand_blocks, first_row // block_len, local_blocks, 1)
    block_ids = jnp.arange(nblocks, dtype=jnp.int32)
    random_hit = jnp.any(chosen[:, :, :, None] == block_ids[None, None, None, :], axis=2)
    random_hit = jnp.broadcast_to(
        random_hit[:, :, None, :, None], (head_count, local_blocks, block_len, nblocks, block_len)
    )
    return always[None] | random_hit.reshape(head_count, local_rows, seq_len)


def score_block(query_heads, key_heads, allowed, score_scale):
    scores = (
        jnp.einsum("sqhd,skhd->shqk", query_heads, key_heads, preferred_element_type=jnp.float32)
        * score_scale
    )
    return jnp.where(allowed, scores, MASKED)


def forward_pass(tokens, seg_full, weights, mask_blocks, first_row):
    w_attn_b, w_out_b, w_up_b, w_down_b, up_bias_b, bias_b, gain_b = weights
    seq_count, local_rows, model_width = tokens.shape
    head_count = mask_blocks.shape[0]
    head_size = model_width // head_count
    score_scale = head_size ** (-0.5)
    bias_f = bias_b.astype(jnp.float32)
    gain_f = gain_b.astype(jnp.float32)
    row_data = tokens.reshape(-1, model_width)
    projected = jnp.dot(row_data, w_attn_b, preferred_element_type=jnp.float32)
    queries = (projected[:, :model_width] + bias_f[0]).astype(jnp.bfloat16)
    keys_loc = projected[:, model_width : 2 * model_width].astype(jnp.bfloat16)
    values_loc = (projected[:, 2 * model_width :] + bias_f[1]).astype(jnp.bfloat16)
    keys_full, values_full = (
        lax.all_gather(
            keys_loc.reshape(seq_count, local_rows, model_width), "seq", axis=1, tiled=True
        ),
        lax.all_gather(
            values_loc.reshape(seq_count, local_rows, model_width), "seq", axis=1, tiled=True
        ),
    )
    seq_len = keys_full.shape[1]
    query_heads = queries.reshape(seq_count, local_rows, head_count, head_size)
    key_heads = keys_full.reshape(seq_count, seq_len, head_count, head_size)
    value_heads = values_full.reshape(seq_count, seq_len, head_count, head_size)
    seg_local = lax.dynamic_slice_in_dim(seg_full, first_row, local_rows, 1)
    allowed = mask_blocks[None] & (seg_local[:, None, :, None] == seg_full[:, None, None, :])
    scores = score_block(query_heads, key_heads, allowed, score_scale)
    row_max = jnp.max(scores, axis=-1, keepdims=True)
    exponent = jnp.exp(scores - row_max)
    row_total = jnp.sum(exponent, axis=-1, keepdims=True)
    attn_probs = exponent / row_total
    log_total = row_max + jnp.log(row_total)
    probs_low = attn_probs.astype(jnp.bfloat16)
    mixture = jnp.einsum(
        "shqk,skhd->sqhd", probs_low, value_heads, preferred_element_type=jnp.float32
    )
    attended = mixture.reshape(-1, model_width).astype(jnp.bfloat16)
    branch = jnp.dot(attended, w_out_b, preferred_element_type=jnp.float32) + bias_f[2]
    first_norm, first_back = jax.vjp(
        layer_norm, row_data.astype(jnp.float32) + branch, gain_f[0], bias_f[4]
    )
    first_low = first_norm.astype(jnp.bfloat16)
    pre_act = jnp.dot(first_low, w_up_b, preferred_element_type=jnp.float32) + up_bias_b.astype(
        jnp.float32
    )
    act_float, gelu_back = jax.vjp(gelu_exact, pre_act)
    activation = act_float.astype(jnp.bfloat16)
    ffn_out = jnp.dot(activation, w_down_b, preferred_element_type=jnp.float32) + bias_f[3]
    result, second_back = jax.vjp(layer_norm, first_norm + ffn_out, gain_f[1], bias_f[5])
    stored = (
        row_data,
        query_heads,
        key_heads,
        value_heads,
        allowed,
        log_total,
        attended,
        first_low,
        activation,
        first_back,
        gelu_back,
        second_back,
    )
    return (result.astype(jnp.bfloat16).reshape(seq_count, local_rows, model_width), stored)


def backward_pass(stored, upstream, weights):
    w_attn_b, w_out_b, w_up_b, w_down_b, up_bias_b, bias_b, gain_b = weights
    (
        row_data,
        query_heads,
        key_heads,
        value_heads,
        allowed,
        log_total,
        attended,
        first_low,
        activation,
        first_back,
        gelu_back,
        second_back,
    ) = stored
    seq_count, local_rows, head_count, head_size = query_heads.shape
    seq_len = key_heads.shape[1]
    model_width = head_count * head_size
    score_scale = head_size ** (-0.5)
    grad_second, grad_gain_two, grad_shift_two = second_back(upstream)
    ffn_grad = grad_second.astype(jnp.bfloat16)
    grad_down = outer_grad(activation, ffn_grad)
    grad_bias_down = col_sums(ffn_grad)
    act_grad = times_transposed(ffn_grad, w_down_b)
    (pre_float,) = gelu_back(act_grad)
    pre_grad = pre_float.astype(jnp.bfloat16)
    grad_up = outer_grad(first_low, pre_grad)
    grad_up_bias = col_sums(pre_grad)
    first_grad = grad_second + times_transposed(pre_grad, w_up_b)
    grad_first, grad_gain_one, grad_shift_one = first_back(first_grad)
    branch_grad = grad_first.astype(jnp.bfloat16)
    grad_out = outer_grad(attended, branch_grad)
    grad_bias_out = col_sums(branch_grad)
    attended_grad = (
        times_transposed(branch_grad, w_out_b)
        .astype(jnp.bfloat16)
        .reshape(seq_count, local_rows, head_count, head_size)
    )
    scores = score_block(query_heads, key_heads, allowed, score_scale)
    attn_probs = jnp.exp(scores - log_total)
    prob_grad = jnp.einsum(
        "sqhd,skhd->shqk", attended_grad, value_heads, preferred_element_type=jnp.float32
    )
    row_dot = jnp.sum(prob_grad * attn_probs, axis=-1, keepdims=True)
    score_grad = (attn_probs * (prob_grad - row_dot)).astype(jnp.bfloat16)
    query_grad = (
        jnp.einsum("shqk,skhd->sqhd", score_grad, key_heads, preferred_element_type=jnp.float32)
        * score_scale
    ).astype(jnp.bfloat16)
    probs_low = attn_probs.astype(jnp.bfloat16)
    value_part = jnp.einsum(
        "shqk,sqhd->skhd", probs_low, attended_grad, preferred_element_type=jnp.float32
    )
    key_part = (
        jnp.einsum("shqk,sqhd->skhd", score_grad, query_heads, preferred_element_type=jnp.float32)
        * score_scale
    )
    key_grad, value_grad = (
        lax.psum_scatter(
            key_part.reshape(seq_count, seq_len, model_width).astype(jnp.bfloat16),
            "seq",
            scatter_dimension=1,
            tiled=True,
        ).astype(jnp.float32),
        lax.psum_scatter(
            value_part.reshape(seq_count, seq_len, model_width).astype(jnp.bfloat16),
            "seq",
            scatter_dimension=1,
            tiled=True,
        ).astype(jnp.float32),
    )
    key_low = key_grad.astype(jnp.bfloat16).reshape(-1, model_width)
    value_low = value_grad.astype(jnp.bfloat16).reshape(-1, model_width)
    query_low = query_grad.reshape(-1, model_width)
    proj_grad = jnp.concatenate([query_low, key_low, value_low], axis=1)
    grad_attn = outer_grad(row_data, proj_grad)
    input_grad = grad_first + times_transposed(proj_grad, w_attn_b)
    grad_biases = jnp.stack(
        [
            col_sums(query_low),
            col_sums(value_low),
            grad_bias_out,
            grad_bias_down,
            grad_shift_one,
            grad_shift_two,
        ]
    )
    grad_gains = jnp.stack([grad_gain_one, grad_gain_two])
    gradients = (grad_attn, grad_out, grad_up, grad_down, grad_up_bias, grad_biases, grad_gains)
    return (input_grad.reshape(seq_count, local_rows, model_width), gradients)


def body(
    block_input,
    cotangent,
    segments,
    rand_blocks,
    w_attn,
    w_out,
    w_up,
    w_down,
    up_bias,
    bias_rows,
    norm_gains,
):
    micro_count, seq_count, local_rows, model_width = block_input.shape
    seq_len = segments.shape[2]
    first_row = lax.axis_index("seq") * local_rows
    mask_blocks = visible_mask(rand_blocks, first_row, local_rows, seq_len)
    masters = (w_attn, w_out, w_up, w_down, up_bias, bias_rows, norm_gains)
    halves = cast_half(masters)
    totals = tuple(
        (
            (
                jnp.zeros((member.shape[0] * lax.axis_size("dp"),) + member.shape[1:], jnp.float32)
                if member.ndim == 1 or (member is not bias_rows and member is not norm_gains)
                else jnp.zeros(
                    (member.shape[0], member.shape[1] * lax.axis_size("dp")), jnp.float32
                )
            )
            for member in masters
        )
    )
    outputs = []
    in_grads = []
    for micro_index in range(micro_count):
        fwd_set = (
            lax.all_gather(halves[0], "dp", axis=0, tiled=True),
            lax.all_gather(halves[1], "dp", axis=0, tiled=True),
            lax.all_gather(halves[2], "dp", axis=0, tiled=True),
            lax.all_gather(halves[3], "dp", axis=0, tiled=True),
            lax.all_gather(halves[4], "dp", axis=0, tiled=True),
            lax.all_gather(halves[5], "dp", axis=1, tiled=True),
            lax.all_gather(halves[6], "dp", axis=1, tiled=True),
        )
        result, stored = forward_pass(
            block_input[micro_index], segments[micro_index], fwd_set, mask_blocks, first_row
        )
        outputs.append(result)
        back_set = (
            lax.all_gather(halves[0], "dp", axis=0, tiled=True),
            lax.all_gather(halves[1], "dp", axis=0, tiled=True),
            lax.all_gather(halves[2], "dp", axis=0, tiled=True),
            lax.all_gather(halves[3], "dp", axis=0, tiled=True),
            lax.all_gather(halves[4], "dp", axis=0, tiled=True),
            lax.all_gather(halves[5], "dp", axis=1, tiled=True),
            lax.all_gather(halves[6], "dp", axis=1, tiled=True),
        )
        upstream = cotangent[micro_index].reshape(-1, model_width).astype(jnp.float32)
        input_grad, gradients = backward_pass(stored, upstream, back_set)
        in_grads.append(input_grad)
        totals = tuple((total_part + grad_part for total_part, grad_part in zip(totals, gradients)))
    shards = (
        lax.psum_scatter(totals[0], "dp", scatter_dimension=0, tiled=True),
        lax.psum_scatter(totals[1], "dp", scatter_dimension=0, tiled=True),
        lax.psum_scatter(totals[2], "dp", scatter_dimension=0, tiled=True),
        lax.psum_scatter(totals[3], "dp", scatter_dimension=0, tiled=True),
        lax.psum_scatter(totals[4], "dp", scatter_dimension=0, tiled=True),
        lax.psum_scatter(totals[5], "dp", scatter_dimension=1, tiled=True),
        lax.psum_scatter(totals[6], "dp", scatter_dimension=1, tiled=True),
    )
    summed = (
        lax.psum(shards[0].astype(jnp.bfloat16), "seq").astype(jnp.float32),
        lax.psum(shards[1].astype(jnp.bfloat16), "seq").astype(jnp.float32),
        lax.psum(shards[2].astype(jnp.bfloat16), "seq").astype(jnp.float32),
        lax.psum(shards[3].astype(jnp.bfloat16), "seq").astype(jnp.float32),
        lax.psum(shards[4].astype(jnp.bfloat16), "seq").astype(jnp.float32),
        lax.psum(shards[5].astype(jnp.bfloat16), "seq").astype(jnp.float32),
        lax.psum(shards[6].astype(jnp.bfloat16), "seq").astype(jnp.float32),
    )
    return (
        jnp.stack(outputs, 0),
        jnp.stack(in_grads, 0),
        summed[0],
        summed[1],
        summed[2],
        summed[3],
        summed[4],
        summed[5],
        summed[6],
    )


def solution(mesh):
    return jax.shard_map(
        body,
        mesh=mesh,
        in_specs=(
            P(None, "dp", "seq", None),
            P(None, "dp", "seq", None),
            P(None, "dp", None),
            P(),
            P("dp", None),
            P("dp", None),
            P("dp", None),
            P("dp", None),
            P("dp"),
            P(None, "dp"),
            P(None, "dp"),
        ),
        out_specs=(
            P(None, "dp", "seq", None),
            P(None, "dp", "seq", None),
            P("dp", None),
            P("dp", None),
            P("dp", None),
            P("dp", None),
            P("dp"),
            P(None, "dp"),
            P(None, "dp"),
        ),
        check_vma=False,
    )
```

profile of v0, /device:TPU:0, one launch (start us, length us, event | category | flops | bytes accessed | tf_op | source)
XLA Modules:
  0.0 952.1 jit_solution(16371674868866285277)
XLA Ops:
  9.3 37.9 %all-gather.16.cloned.1.call-done = bf16[768,2304]{1,0:T(8,128)(2,1)} async-done(((bf16[96,2304]{1,0:T(8,128)(2,1)}), bf16[768,2304]{1,0:T(8,128)(2,1)}) %all-gather.16.cloned.1.call-update) | async-done | bytes 3538960 | tf_op jit(solution)/shard_map/all_gather | solution.py:263
  52.7 8.9 all-gather.4
  80.5 8.8 all-gather.6
  93.9 17.3 %reshape.625 = pred[12,256,1024]{2,1,0:T(32,128)(4,1)} reshape(pred[12,4,64,16,64]{4,3,2,1,0:T(8,128)(4,1)} %broadcast_in_dim.25) | data formatting | bytes 6291456 | tf_op jit(solution)/shard_map/reshape | solution.py:57
  137.7 15.0 %all-gather.18.cloned.1.call-done = bf16[768,768]{1,0:T(8,128)(2,1)} async-done(((bf16[96,768]{1,0:T(8,128)(2,1)}), bf16[768,768]{1,0:T(8,128)(2,1)}) %all-gather.18.cloned.1.call-update) | async-done | bytes 1179664 | tf_op jit(solution)/shard_map/all_gather | solution.py:264
  154.8 39.1 %all-gather.20.cloned.1.call-done = bf16[768,3072]{1,0:T(8,128)(2,1)} async-done(((bf16[96,3072]{1,0:T(8,128)(2,1)}), bf16[768,3072]{1,0:T(8,128)(2,1)}) %all-gather.20.cloned.1.call-update) | async-done | bytes 4718608 | tf_op jit(solution)/shard_map/all_gather | solution.py:265
  194.0 11.6 %multiply_convert_fusion.4 = (bf16[256,3072]{1,0:T(8,128)(2,1)}, f32[256,3072]{1,0:T(8,128)}, f32[256,3072]{1,0:T(8,128)}) fusion(f32[3072]{0:T(1024)S(1)} %bitcast.239, bf16[768,3072]{1,0:T(8,128)(2,1)} %all-gather.20.cloned.1.call-done, f32[256,768]{1,0:T(8,128)S(1)} %get-tuple-element.135, f32[256]{0:T(256)S(1)} %fusion.79, ...), kind=kOutput, calls=%fused_computation.37 | convolution fusion | flops 1260847104 | bytes 13389824 | tf_op jit(solution)/shard_map/dot_general | solution.py:111
  205.6 29.6 %all-gather.22.cloned.1.call-done = bf16[3072,768]{1,0:T(8,128)(2,1)} async-done(((bf16[384,768]{1,0:T(8,128)(2,1)}), bf16[3072,768]{1,0:T(8,128)(2,1)}) %all-gather.22.cloned.1.call-update) | async-done | bytes 4718608 | tf_op jit(solution)/shard_map/all_gather | solution.py:266
  239.6 34.9 %all-gather.26.cloned.1.call-done = bf16[1024,768]{1,0:T(8,128)(2,1)} async-done(((bf16[256,768]{1,0:T(8,128)(2,1)}), bf16[1024,768]{1,0:T(8,128)(2,1)}) %all-gather.26.cloned.1.call-update) | async-done | bytes 1572880 | tf_op jit(solution)/shard_map/all_gather | solution.py:82
  288.7 23.9 %all-gather.24.cloned.1.call-done = bf16[1024,768]{1,0:T(8,128)(2,1)} async-done(((bf16[256,768]{1,0:T(8,128)(2,1)}), bf16[1024,768]{1,0:T(8,128)(2,1)}) %all-gather.24.cloned.1.call-update) | async-done | bytes 1572880 | tf_op jit(solution)/shard_map/all_gather | solution.py:85
  322.7 11.6 %multiply_convert_fusion.5 = (bf16[256,3072]{1,0:T(8,128)(2,1)S(1)}, f32[256,3072]{1,0:T(8,128)S(1)}, f32[256,3072]{1,0:T(8,128)}) fusion(f32[3072]{0:T(1024)S(1)} %bitcast.240, bf16[768,3072]{1,0:T(8,128)(2,1)} %all-gather.20.cloned.1.call-done, f32[256,768]{1,0:T(8,128)S(1)} %get-tuple-element.128, f32[768]{0:T(1024)S(1)} %get-tuple-element.70, ...), kind=kOutput, calls=%fused_computation.50 | convolution fusion | flops 1260847104 | bytes 13389824 | tf_op jit(solution)/shard_map/dot_general | solution.py:111
  352.8 8.1 fusion.24
  436.9 31.9 %reduce-scatter.23.cloned.1.call-done = bf16[1,256,768]{1,2,0:T(8,128)(2,1)} async-done(((bf16[1,1024,768]{1,2,0:T(8,128)(2,1)}), bf16[1,256,768]{1,2,0:T(8,128)(2,1)}) %reduce-scatter.23.cloned.1.call-update) | async-done | bytes 393232 | tf_op jit(solution)/shard_map/reduce_scatter | solution.py:200
  468.8 36.4 %reduce-scatter.21.cloned.1.call-done = bf16[1,256,768]{1,2,0:T(8,128)(2,1)} async-done(((bf16[1,1024,768]{1,2,0:T(8,128)(2,1)}), bf16[1,256,768]{1,2,0:T(8,128)(2,1)}) %reduce-scatter.21.cloned.1.call-update) | async-done | bytes 393232 | tf_op jit(solution)/shard_map/reduce_scatter | solution.py:194
  512.6 8.2 copy.84
  541.6 8.5 reduce-scatter.25.cloned.1.call-done
  551.7 67.7 %reduce-scatter.31.cloned.1.call-done = f32[96,2304]{1,0:T(8,128)} async-done(((f32[768,2304]{1,0:T(8,128)}), f32[96,2304]{1,0:T(8,128)}) %reduce-scatter.31.cloned.1.call-update) | async-done | bytes 884752
  621.6 77.6 %reduce-scatter.27.cloned.1.call-done = f32[96,3072]{1,0:T(8,128)} async-done(((f32[768,3072]{1,0:T(8,128)}), f32[96,3072]{1,0:T(8,128)}) %reduce-scatter.27.cloned.1.call-update) | async-done | bytes 1179664 | tf_op jit(solution)/shard_map/reduce_scatter | solution.py:291
  701.4 77.7 %reduce-scatter.29.cloned.1.call-done = f32[384,768]{1,0:T(8,128)} async-done(((f32[3072,768]{1,0:T(8,128)}), f32[384,768]{1,0:T(8,128)}) %reduce-scatter.29.cloned.1.call-update) | async-done | bytes 1179664 | tf_op jit(solution)/shard_map/reduce_scatter | solution.py:292
  782.5 23.1 %all-reduce = bf16[3072]{0:T(1024)(128)(2,1)S(1)} all-reduce(f32[3072]{0:T(1024)S(1)} %add.337), channel_id=14, replica_groups=mesh['dp'=8,'seq'=4] {'dp'}, use_global_device_ids=true, to_apply=%region_37.38.clone | all-reduce | flops 3072 | bytes 18432
  806.7 9.8 %reduce-scatter.35.cloned.1.call-done = f32[96,2]{1,0:T(8,128)} async-done(((f32[768,2]{1,0:T(8,128)}), f32[96,2]{1,0:T(8,128)}) %reduce-scatter.35.cloned.1.call-update) | async-done | bytes 784
  823.2 30.0 %reduce-scatter.33.cloned.1.call-done = f32[96,6]{1,0:T(8,128)} async-done(((f32[768,6]{1,0:T(8,128)}), f32[96,6]{1,0:T(8,128)}) %reduce-scatter.33.cloned.1.call-update) | async-done | bytes 2320
  854.1 11.8 %all-reduce.1 = (bf16[384]{0:T(512)(128)(2,1)S(1)}, bf16[6,96]{1,0:T(8,128)(2,1)S(1)}, bf16[2,96]{1,0:T(2,128)(2,1)S(1)}) all-reduce(bf16[384]{0:T(512)(128)(2,1)S(1)} %dynamic-slice.5, bf16[6,96]{1,0:T(8,128)(2,1)S(1)} %copy.87, bf16[2,96]{1,0:T(2,128)(2,1)S(1)} %copy.89), channel_id=1, replica_groups=mesh['dp'=8,'seq'=4] {'seq'}, use_global_device_ids=true, to_apply=%region_38.39 | all-reduce | flops 1152 | bytes 4608 | tf_op jit(solution)/shard_map/psum | solution.py:302
  867.7 70.5 %all-reduce.5.cloned.1.call-done = (bf16[96,2304]{0,1:T(8,128)(2,1)}, bf16[96,768]{1,0:T(8,128)(2,1)}, bf16[96,3072]{1,0:T(8,128)(2,1)}, bf16[384,768]{1,0:T(8,128)(2,1)}) async-done(((bf16[96,2304]{0,1:T(8,128)(2,1)}, bf16[96,768]{1,0:T(8,128)(2,1)}, bf16[96,3072]{1,0:T(8,128)(2,1)}, bf16[384,768]{1,0:T(8,128)(2,1)}), (bf16[96,2304]{0,1:T(8,128)(2,1)}, bf16[96,768]{1,0:T(8,128)(2,1)}, ...) | async-done | bytes 1769488 | tf_op jit(solution)/shard_map/psum | solution.py:298
  (314 shorter events, 235.9 us)
Async XLA Ops:
  7.2 40.0 %all-gather.16.cloned.1.call-start = ((), (), s32[]{:S(2)}) async-start(), calls=%async_computation.10 | async-start | bytes 3981312 | tf_op jit(solution)/shard_map/all_gather | solution.py:263
  9.3 104.4 %all-gather.30.cloned.1.call-start = ((), (), s32[]{:S(2)}) async-start(), calls=%async_computation.24 | async-start | bytes 1966080 | tf_op jit(solution)/shard_map/all_gather | solution.py:82
  52.6 76.6 %all-gather.28.cloned.1.call-start = ((), (), s32[]{:S(2)}) async-start(), calls=%async_computation.23 | async-start | bytes 1966080 | tf_op jit(solution)/shard_map/all_gather | solution.py:85
  66.3 86.4 %all-gather.18.cloned.1.call-start = ((), (), s32[]{:S(2)}) async-start(), calls=%async_computation.11 | async-start | bytes 1327104 | tf_op jit(solution)/shard_map/all_gather | solution.py:264
  67.1 126.9 %all-gather.20.cloned.1.call-start = ((), (), s32[]{:S(2)}) async-start(), calls=%async_computation.12 | async-start | bytes 5308416 | tf_op jit(solution)/shard_map/all_gather | solution.py:265
  69.3 165.9 %all-gather.22.cloned.1.call-start = ((), (), s32[]{:S(2)}) async-start(), calls=%async_computation.13 | async-start | bytes 5308416 | tf_op jit(solution)/shard_map/all_gather | solution.py:266
  71.6 202.9 %all-gather.26.cloned.1.call-start = ((), (), s32[]{:S(2)}) async-start(), calls=%async_computation.22 | async-start | bytes 1966080 | tf_op jit(solution)/shard_map/all_gather | solution.py:82
  72.4 240.2 %all-gather.24.cloned.1.call-start = ((), (), s32[]{:S(2)}) async-start(), calls=%async_computation.21 | async-start | bytes 1966080 | tf_op jit(solution)/shard_map/all_gather | solution.py:85
  113.3 164.0 %copy-start.17 = (bf16[256,768]{0,1:T(8,128)(2,1)}, bf16[256,768]{0,1:T(8,128)(2,1)S(1)}, u32[]{:S(2)}) copy-start(bf16[256,768]{0,1:T(8,128)(2,1)S(1)} %copy.75) | copy-start | bytes 1179652
  113.3 311.8 %reduce-scatter.19.cloned.1.call-start = ((), (), s32[]{:S(2)}) async-start(), calls=%async_computation.15 | async-start | bytes 1966080 | tf_op jit(solution)/shard_map/reduce_scatter | solution.py:200
  360.9 70.7 %reduce-scatter.17.cloned.1.call-start = ((), (), s32[]{:S(2)}) async-start(), calls=%async_computation.14 | async-start | bytes 1966080 | tf_op jit(solution)/shard_map/reduce_scatter | solution.py:194
  377.5 91.3 %reduce-scatter.23.cloned.1.call-start = ((), (), s32[]{:S(2)}) async-start(), calls=%async_computation.17 | async-start | bytes 1966080 | tf_op jit(solution)/shard_map/reduce_scatter | solution.py:200
  391.4 113.8 %reduce-scatter.21.cloned.1.call-start = ((), (), s32[]{:S(2)}) async-start(), calls=%async_computation.16 | async-start | bytes 1966080 | tf_op jit(solution)/shard_map/reduce_scatter | solution.py:194
  408.3 141.8 %reduce-scatter.25.cloned.1.call-start = ((), (), s32[]{:S(2)}) async-start(), calls=%async_computation.18 | async-start | bytes 2654208 | tf_op jit(solution)/shard_map/reduce_scatter | solution.py:290
  412.8 206.6 %reduce-scatter.31.cloned.1.call-start = ((), (), s32[]{:S(2)}) async-start(), calls=%async_computation.25 | async-start | bytes 7962624
  520.9 178.3 %reduce-scatter.27.cloned.1.call-start = ((), (), s32[]{:S(2)}) async-start(), calls=%async_computation.19 | async-start | bytes 10616832 | tf_op jit(solution)/shard_map/reduce_scatter | solution.py:291
  529.3 249.7 %reduce-scatter.29.cloned.1.call-start = ((), (), s32[]{:S(2)}) async-start(), calls=%async_computation.20 | async-start | bytes 10616832 | tf_op jit(solution)/shard_map/reduce_scatter | solution.py:292
  538.4 278.1 %reduce-scatter.35.cloned.1.call-start = ((), (), s32[]{:S(2)}) async-start(), calls=%async_computation.27 | async-start | bytes 442368
  539.9 313.4 %reduce-scatter.33.cloned.1.call-start = ((), (), s32[]{:S(2)}) async-start(), calls=%async_computation.26 | async-start | bytes 442368
  541.6 396.6 %all-reduce.5.cloned.1.call-start = ((), (), s32[]{:S(2)}) async-start(), calls=%async_computation.28 | async-start | bytes 3833856 | tf_op jit(solution)/shard_map/psum | solution.py:298
  551.7 229.6 %copy-start.53 = (u32[32]{0:T(128)S(1)}, u32[32]{0:T(128)}, u32[]{:S(2)}) copy-start(u32[32]{0:T(128)} %constant.157) | copy-start | bytes 388
  621.6 184.1 %copy-start.34 = (bf16[1,1,256,768]{3,2,1,0:T(8,128)(2,1)S(1)}, bf16[1,1,256,768]{3,2,1,0:T(8,128)(2,1)}, u32[]{:S(2)}) copy-start(bf16[1,1,256,768]{3,2,1,0:T(8,128)(2,1)} %get-tuple-element.112) | copy-start | bytes 1179652
  621.6 184.1 %copy-start.35 = (bf16[1,1,256,768]{3,2,1,0:T(8,128)(2,1)S(1)}, bf16[1,1,256,768]{3,2,1,0:T(8,128)(2,1)}, u32[]{:S(2)}) copy-start(bf16[1,1,256,768]{3,2,1,0:T(8,128)(2,1)} %get-tuple-element.113) | copy-start | bytes 1179652
  822.0 123.4 %copy-start.1 = (s32[12,16,3]{1,2,0:T(4,128)S(1)}, s32[12,16,3]{1,2,0:T(4,128)}, u32[]{:S(2)}) copy-start(s32[12,16,3]{1,2,0:T(4,128)} %param.14) | copy-start | bytes 6916
  (56 other events, 882.0 us)
Sparse Core Ops, SparseCore 0:
  10.5 36.6 all-gather.15
  52.8 37.0 all-gather.29
  92.0 35.9 all-gather.27
  129.8 22.9 all-gather.17
  155.0 38.9 all-gather.19
  196.3 38.9 all-gather.21
  237.4 37.0 all-gather.25
  276.6 35.9 all-gather.23
  361.0 34.1 reduce-scatter.18
  397.3 34.2 reduce-scatter.16
  434.5 34.2 reduce-scatter.22
  471.0 34.2 reduce-scatter.20
  508.6 41.4 reduce-scatter.24
  553.9 65.4 reduce-scatter.30
  622.7 76.4 reduce-scatter.26
  702.6 76.4 reduce-scatter.28
  782.6 33.8 reduce-scatter.34
  819.4 33.8 reduce-scatter.32
  856.4 81.6 all-reduce.4
where the time goes:
time: 959 us; the launch traced here: 952 us
  waiting for transfers between devices  597 us (62%)
  matrix products  162 us (17%)
  local copies, waits for them, and re-layouts  64.6 us (7%)
  blocking collectives  60.5 us (6%)
  other arithmetic  50 us (5%)
  between operations  16.1 us (2%)
    unnamed x22, waiting for transfers between devices  108 us
    reduce_scatter x1, waiting for transfers between devices, body(): lax.psum_scatter(totals[3], 'dp', scatter_dimension=0, tiled=True)  77.7 us
    reduce_scatter x1, waiting for transfers between devices, body(): lax.psum_scatter(totals[2], 'dp', scatter_dimension=0, tiled=True)  77.6 us
    psum x1, waiting for transfers between devices, body(): lax.psum(shards[0].astype(jnp.bfloat16), 'seq').astype(jnp.float32)  70.5 us
    reduce_scatter x2, waiting for transfers between devices, backward_pass(): lax.psum_scatter(key_part.reshape(seq_count, seq_len, model_width).astype...  42.9 us
    all_gather x1, waiting for transfers between devices, body(): lax.all_gather(halves[2], 'dp', axis=0, tiled=True)  39.1 us
    all_gather x1, waiting for transfers between devices, body(): lax.all_gather(halves[0], 'dp', axis=0, tiled=True)  37.9 us
    all_gather x2, waiting for transfers between devices, forward_pass(): lax.all_gather(keys_loc.reshape(seq_count, local_rows, model_width), 'seq...  35 us
  transfers between devices with their start and end apart: 19, of which 16 were waited for; matrix products, arithmetic and copies ran while one was open for 22% of the time, Pallas kernels for 0%

commit v1 on v0

v1 whole, which is shorter than its diff:
```python
import jax
import jax.numpy as jnp
from jax import lax
from jax.sharding import PartitionSpec as P

EPSILON = 1e-05
MASKED = -1e30
GROUP = 8
BOTH = ("dp", "seq")
F32 = jnp.float32
BF16 = jnp.bfloat16


def layer_norm(tensor, gain_row, offset):
    centre = tensor - jnp.mean(tensor, axis=-1, keepdims=True)
    spread = jnp.mean(centre * centre, axis=-1, keepdims=True)
    return centre * lax.rsqrt(spread + EPSILON) * gain_row + offset


def gelu_exact(tensor):
    return jax.nn.gelu(tensor, approximate=False)


def col_sums(tensor):
    return jnp.sum(tensor.astype(F32), axis=0)


def outer_grad(left, right):
    return lax.dot_general(left, right, (((0,), (0,)), ((), ())), preferred_element_type=F32)


def times_transposed(left, right):
    return lax.dot_general(left, right, (((1,), (1,)), ((), ())), preferred_element_type=F32)


def swap(value, axis, bit):
    size = lax.axis_size(axis)
    return lax.ppermute(value, axis, [(i, i ^ bit) for i in range(size)])


def gather_chunks(mine):
    rows = mine.shape[0]
    half = rows // 32 * 16
    first = swap(mine, "dp", 2)
    second = swap(mine, "dp", 4)
    low = swap(first[:half], "dp", 4)
    high = swap(second[half:], "dp", 2)
    even = jnp.stack([mine, first, second, jnp.concatenate([low, high])])
    odd = swap(even, "dp", 1)
    full = jnp.stack([even, odd], axis=1).reshape((GROUP,) + mine.shape)
    bit = GROUP
    while bit < lax.axis_size("dp"):
        full = jnp.concatenate([full, swap(full, "dp", bit)])
        bit *= 2
    return full


def by_owner(chunks):
    own = lax.axis_index("dp")
    return jnp.stack(
        [lax.dynamic_index_in_dim(chunks, own ^ k, 0, False) for k in range(chunks.shape[0])]
    )


def reduce_chunks(chunks):
    bit = chunks.shape[0] // 2
    while bit >= GROUP:
        other = swap(chunks[bit:].astype(BF16), "dp", bit)
        chunks = chunks[:bit] + other.astype(F32)
        bit //= 2
    rows = chunks.shape[1]
    half = rows // 32 * 16
    pairs = chunks.reshape((4, 2) + chunks.shape[1:])
    plane = pairs[:, 0] + swap(pairs[:, 1].astype(BF16), "dp", 1).astype(F32)
    diagonal = plane[3].astype(BF16)
    to_second = swap(diagonal[:half], "dp", 2).astype(F32)
    to_first = swap(diagonal[half:], "dp", 4).astype(F32)
    second = jnp.concatenate([plane[2, :half] + to_second, plane[2, half:]])
    first = jnp.concatenate([plane[1, :half], plane[1, half:] + to_first])
    total = plane[0] + swap(first.astype(BF16), "dp", 2).astype(F32)
    total = total + swap(second.astype(BF16), "dp", 4).astype(F32)
    low, high = total[:half].astype(BF16), total[half:].astype(BF16)
    low_other, high_other = swap(low, "seq", 1), swap(high, "seq", 3)
    low = (low.astype(F32) + low_other.astype(F32)).astype(BF16)
    high = (high.astype(F32) + high_other.astype(F32)).astype(BF16)
    low_other, high_other = swap(low, "seq", 3), swap(high, "seq", 1)
    return jnp.concatenate(
        [low.astype(F32) + low_other.astype(F32), high.astype(F32) + high_other.astype(F32)]
    )


def route(which):
    size, ring = lax.axis_size("dp"), lax.axis_size("seq")
    pairs = []
    for index in range(size):
        for place in range(ring):
            to_dp = (index & ~1) | (place >> 1)
            to_seq = 2 * ((place & 1) ^ which) + (index & 1)
            pairs.append((index * ring + place, to_dp * ring + to_seq))
    return pairs


def to_chip(slabs, place):
    parts = []
    for which in range(2):
        slab = lax.dynamic_index_in_dim(slabs, (place & 1) ^ which, 0, False)
        parts.append(lax.ppermute(slab, BOTH, route(which)))
    return jnp.concatenate(parts)


def from_chip(rows, place):
    half = rows.shape[0] // 2
    parts = []
    for which in range(2):
        back = [(target, source) for source, target in route(which)]
        parts.append(lax.ppermute(rows[which * half : (which + 1) * half], BOTH, back))
    parts = jnp.stack(parts)
    return jnp.where((place & 1) == 0, parts, parts[::-1])


def body(
    block_input,
    cotangent,
    segments,
    rand_blocks,
    w_attn,
    w_out,
    w_up,
    w_down,
    up_bias,
    bias_rows,
    norm_gains,
):
    micro, _, quarter, width = block_input.shape
    ring, size = lax.axis_size("seq"), lax.axis_size("dp")
    assert ring == 2 * micro and block_input.shape[1] == 1 and size % GROUP == 0
    heads, nblocks = rand_blocks.shape[:2]
    length = segments.shape[2]
    block = length // nblocks
    rows = 2 * quarter
    head = width // heads
    scale = head ** (-0.5)
    own, place = lax.axis_index("dp"), lax.axis_index("seq")
    core = own & 1

    tokens = to_chip(block_input[:, 0], place)
    upstream = to_chip(cotangent[:, 0], place).astype(F32)
    seg_own = segments[:, 0]
    seg_other = swap(seg_own, "dp", 1)
    seg = jnp.where((place & 1) == core, seg_own, seg_other)
    seg = lax.dynamic_index_in_dim(seg, place >> 1, 0, False).reshape(ring, quarter)
    per = quarter // block
    flip = place >> 1
    quarters = [2 * core + flip, 2 * core + 1 - flip, 2 * (1 - core) + flip, 2 * (1 - core) + 1 - flip]
    pick = lambda table, axis, wanted: jnp.concatenate(
        [lax.dynamic_index_in_dim(table, item, axis, False) for item in wanted], axis
    )
    key_blocks = jnp.concatenate([item * per + jnp.arange(per, dtype=jnp.int32) for item in quarters])
    query_blocks = key_blocks[: nblocks // 2]
    seg_key = pick(seg, 0, quarters)
    seg_query = seg_key[:rows]
    rand_query = pick(rand_blocks.reshape(heads, ring, per, -1), 1, quarters[:2])
    q_id, k_id = query_blocks[:, None], key_blocks[None]
    always = (jnp.abs(q_id - k_id) <= 1) | (q_id == 0) | (q_id == nblocks - 1) | (k_id == 0) | (k_id == nblocks - 1)
    hit = jnp.any(rand_query[:, :, :, None] == key_blocks[None, None, None, :], axis=2)
    seen = always[None] | hit
    seen = jnp.broadcast_to(
        seen[:, :, None, :, None], (heads, nblocks // 2, block, nblocks, block)
    ).reshape(heads, rows, length)
    allowed = seen & (seg_query[:, None] == seg_key[None, :])[None]

    part = width // size
    wide = w_up.shape[1]
    pack = lambda member: member.astype(BF16).reshape(part, -1, width).swapaxes(0, 1).reshape(-1, width)
    small = jnp.concatenate([bias_rows.reshape(-1), norm_gains.reshape(-1), up_bias])
    smalls = small.shape[0]
    small_rows = -(-smalls // (16 * width)) * 16
    small = jnp.pad(small, (0, small_rows * width - smalls)).astype(BF16).reshape(small_rows, width)
    n_attn, n_up, n_down = 3 * part, wide // width * part, wide // size
    group_one = by_owner(gather_chunks(jnp.concatenate([pack(w_attn), small])))
    group_two = by_owner(
        gather_chunks(jnp.concatenate([w_out.astype(BF16), pack(w_up), w_down.astype(BF16)]))
    )
    unpack = lambda chunks: chunks.reshape(size, -1, part, width).swapaxes(1, 2).reshape(size * part, -1)
    w_attn_b = unpack(group_one[:, :n_attn])
    flat = group_one[:, n_attn:].reshape(size, -1).astype(F32)
    bias_f = flat[:, : 6 * part].reshape(size, 6, part).swapaxes(0, 1).reshape(6, width)
    gain_f = flat[:, 6 * part : 8 * part].reshape(size, 2, part).swapaxes(0, 1).reshape(2, width)
    up_bias_f = flat[:, 8 * part : 8 * part + wide // size].reshape(-1)
    w_out_b = group_two[:, :part].reshape(width, width)
    w_up_b = unpack(group_two[:, part : part + n_up])
    w_down_b = group_two[:, part + n_up :].reshape(wide, width)

    projected = jnp.dot(tokens, w_attn_b, preferred_element_type=F32)
    queries = (projected[:, :width] + bias_f[0]).astype(BF16)
    keys = projected[:, width : 2 * width].astype(BF16)
    values = (projected[:, 2 * width :] + bias_f[1]).astype(BF16)
    pair = jnp.stack([keys, values])
    pair = jnp.concatenate([pair, swap(pair, "dp", 1)], axis=1)
    query_heads = queries.reshape(rows, heads, head)
    key_heads = pair[0].reshape(length, heads, head)
    value_heads = pair[1].reshape(length, heads, head)
    scores = jnp.einsum("qhd,khd->hqk", query_heads, key_heads, preferred_element_type=F32) * scale
    scores = jnp.where(allowed, scores, MASKED)
    row_max = jnp.max(scores, axis=-1, keepdims=True)
    exponent = jnp.exp(scores - row_max)
    row_total = jnp.sum(exponent, axis=-1, keepdims=True)
    attn_probs = exponent / row_total
    log_total = row_max + jnp.log(row_total)
    mixture = jnp.einsum("hqk,khd->qhd", attn_probs.astype(BF16), value_heads, preferred_element_type=F32)
    attended = mixture.reshape(rows, width).astype(BF16)
    branch = jnp.dot(attended, w_out_b, preferred_element_type=F32) + bias_f[2]
    first_norm, first_back = jax.vjp(layer_norm, tokens.astype(F32) + branch, gain_f[0], bias_f[4])
    first_low = first_norm.astype(BF16)
    pre_act = jnp.dot(first_low, w_up_b, preferred_element_type=F32) + up_bias_f
    act_float, gelu_back = jax.vjp(gelu_exact, pre_act)
    activation = act_float.astype(BF16)
    ffn_out = jnp.dot(activation, w_down_b, preferred_element_type=F32) + bias_f[3]
    result, second_back = jax.vjp(layer_norm, first_norm + ffn_out, gain_f[1], bias_f[5])
    output = from_chip(result.astype(BF16), place)

    grad_second, grad_gain_two, grad_shift_two = second_back(upstream)
    ffn_grad = grad_second.astype(BF16)
    grad_down = outer_grad(activation, ffn_grad)
    act_grad = times_transposed(ffn_grad, w_down_b)
    (pre_float,) = gelu_back(act_grad)
    pre_grad = pre_float.astype(BF16)
    grad_up = outer_grad(first_low, pre_grad)
    pack_up = lambda grad: grad.reshape(size, part, -1, width).swapaxes(1, 2).reshape(size, -1, width)
    sum_two = reduce_chunks(
        by_owner(jnp.concatenate([pack_up(grad_up), grad_down.reshape(size, -1, width)], axis=1))
    )

    first_grad = grad_second + times_transposed(pre_grad, w_up_b)
    grad_first, grad_gain_one, grad_shift_one = first_back(first_grad)
    branch_grad = grad_first.astype(BF16)
    grad_out = outer_grad(attended, branch_grad)
    attended_grad = times_transposed(branch_grad, w_out_b).astype(BF16).reshape(rows, heads, head)
    attn_probs = jnp.exp(scores - log_total)
    prob_grad = jnp.einsum("qhd,khd->hqk", attended_grad, value_heads, preferred_element_type=F32)
    row_dot = jnp.sum(prob_grad * attn_probs, axis=-1, keepdims=True)
    score_grad = (attn_probs * (prob_grad - row_dot)).astype(BF16)
    query_low = (
        jnp.einsum("hqk,khd->qhd", score_grad, key_heads, preferred_element_type=F32) * scale
    ).astype(BF16).reshape(rows, width)
    value_part = jnp.einsum("hqk,qhd->khd", attn_probs.astype(BF16), attended_grad, preferred_element_type=F32)
    key_part = jnp.einsum("hqk,qhd->khd", score_grad, query_heads, preferred_element_type=F32) * scale
    parts = jnp.stack([key_part.reshape(length, width), value_part.reshape(length, width)])
    parts = (parts[:, :rows] + swap(parts[:, rows:].astype(BF16), "dp", 1).astype(F32)).astype(BF16)
    key_low, value_low = parts[0], parts[1]
    proj_grad = jnp.concatenate([query_low, key_low, value_low], axis=1)
    grad_attn = outer_grad(tokens, proj_grad)
    input_grad = grad_first + times_transposed(proj_grad, w_attn_b)
    input_grad = from_chip(input_grad.astype(BF16), place).astype(F32)
    grad_biases = jnp.stack(
        [
            col_sums(query_low),
            col_sums(value_low),
            col_sums(branch_grad),
            col_sums(ffn_grad),
            grad_shift_one,
            grad_shift_two,
            grad_gain_one,
            grad_gain_two,
        ]
    )
    small_grad = jnp.concatenate(
        [
            grad_biases.reshape(8, size, part).swapaxes(0, 1).reshape(size, -1),
            col_sums(pre_grad).reshape(size, -1),
        ],
        axis=1,
    )
    small_grad = jnp.pad(small_grad, ((0, 0), (0, small_rows * width - smalls)))
    sum_one = reduce_chunks(
        by_owner(
            jnp.concatenate(
                [
                    pack_up(grad_attn),
                    grad_out.reshape(size, part, width),
                    small_grad.reshape(size, small_rows, width),
                ],
                axis=1,
            )
        )
    )
    unpack_own = lambda total: total.reshape(-1, part, width).swapaxes(0, 1).reshape(part, -1)
    small_sum = sum_one[n_attn + part :].reshape(-1)
    return (
        output[:, None],
        input_grad[:, None],
        unpack_own(sum_one[:n_attn]),
        sum_one[n_attn : n_attn + part],
        unpack_own(sum_two[:n_up]),
        sum_two[n_up:],
        small_sum[8 * part : 8 * part + wide // size],
        small_sum[: 6 * part].reshape(6, part),
        small_sum[6 * part : 8 * part].reshape(2, part),
    )


def solution(mesh):
    return jax.shard_map(
        body,
        mesh=mesh,
        in_specs=(
            P(None, "dp", "seq", None),
            P(None, "dp", "seq", None),
            P(None, "dp", None),
            P(),
            P("dp", None),
            P("dp", None),
            P("dp", None),
            P("dp", None),
            P("dp"),
            P(None, "dp"),
            P(None, "dp"),
        ),
        out_specs=(
            P(None, "dp", "seq", None),
            P(None, "dp", "seq", None),
            P("dp", None),
            P("dp", None),
            P("dp", None),
            P("dp", None),
            P("dp"),
            P(None, "dp"),
            P(None, "dp"),
        ),
        check_vma=False,
    )
```

time: 959 us -> 595 us (0.62)
  waiting for transfers between devices: 597 us -> 104 us
  local copies, waits for them, and re-layouts: 64.6 us -> 165 us
  starting transfers between devices: 1.66 us -> 77.8 us
  blocking collectives: 60.5 us -> 0 us
  other arithmetic: 50 us -> 104 us
  matrix products: 162 us -> 131 us
  between operations: 16.1 us -> 2.6 us
    reduce_scatter x7 -> x0, waiting for transfers between devices: 239 us -> none  [the longest x1 77.7 us: body(): lax.psum_scatter(totals[3], 'dp', scatter_dimension=0, tiled=True)]
    all_gather x8 -> x0, waiting for transfers between devices: 181 us -> none  [the longest x1 39.1 us: body(): lax.all_gather(halves[2], 'dp', axis=0, tiled=True)]
    unnamed x22 -> x0, waiting for transfers between devices: 108 us -> none
    ppermute x0 -> x39, waiting for transfers between devices: none -> 104 us  [the longest x31 104 us: swap(): return lax.ppermute(value, axis, [(i, i ^ bit) for i in range(size)])]
    ppermute x0 -> x39, starting transfers between devices: none -> 77.8 us  [the longest x31 59.6 us: swap(): return lax.ppermute(value, axis, [(i, i ^ bit) for i in range(size)])]
    psum x1 -> x0, waiting for transfers between devices: 70.5 us -> none  [body(): lax.psum(shards[0].astype(jnp.bfloat16), 'seq').astype(jnp.float32)]
    reshape x9 -> x20, local copies, waits for them, and re-layouts: 17.4 us -> 80.6 us  [the longest x1 33.1 us: body(): seen = jnp.broadcast_to(seen[:, :, None, :, None], (heads, nblocks // 2,...]
    another operation x2 -> x23, other arithmetic: 2.19 us -> 46.7 us  [the longest x1 1.25 us: body(): jnp.stack(in_grads, 0)]
  transfers between devices with their start and end apart: 19 -> 39, of which waited for: 16 -> 12; matrix products, arithmetic and copies ran while one was open for 22% -> 49% of each run, Pallas kernels for 0% -> 0%
where the time goes in v1:
time: 595 us; the launch traced here: 584 us
  local copies, waits for them, and re-layouts  165 us (28%)
  matrix products  131 us (22%)
  other arithmetic  104 us (17%)
  waiting for transfers between devices  104 us (17%)
  starting transfers between devices  77.8 us (13%)
    ppermute x31, waiting for transfers between devices, swap(): return lax.ppermute(value, axis, [(i, i ^ bit) for i in range(size)])  104 us
    ppermute x31, starting transfers between devices, swap(): return lax.ppermute(value, axis, [(i, i ^ bit) for i in range(size)])  59.6 us
    reshape x1, local copies, waits for them, and re-layouts, body(): seen = jnp.broadcast_to(seen[:, :, None, :, None], (heads, nblocks // 2,...  33.1 us
    reshape x3, local copies, waits for them, and re-layouts, body(): grad.reshape(size, part, -1, width).swapaxes(1, 2).reshape(size, -1, width)  28.3 us
    another operation x11, other arithmetic  26.2 us
    unnamed x156, local copies, waits for them, and re-layouts  23.1 us
    dot_general x4, matrix products, outer_grad(): lax.dot_general(left, right, (((0,), (0,)), ((), ())), preferred_element_...  21.6 us
    dot_general x1, matrix products, body(): jnp.einsum('qhd,khd->hqk', attended_grad, value_heads, preferred_element_...  19.9 us
  transfers between devices with their start and end apart: 39, of which 12 were waited for; matrix products, arithmetic and copies ran while one was open for 49% of the time, Pallas kernels for 0%

profile of v1, /device:TPU:0, one launch (start us, length us, event | category | flops | bytes accessed | tf_op | source)
XLA Modules:
  0.0 584.1 jit_solution(3297719718152078928)
XLA Ops:
  9.3 9.2 %collective-permute-done.3 = bf16[304,768]{1,0:T(8,128)(2,1)S(1)} collective-permute-done((bf16[304,768]{1,0:T(8,128)(2,1)S(1)}, bf16[304,768]{1,0:T(8,128)(2,1)S(1)}, u32[]{:S(2)}, u32[]{:S(2)}) %collective-permute-start.3) | collective-permute-done | bytes 466976 | tf_op jit(solution)/shard_map/ppermute | solution.py:38
  40.6 14.7 %collective-permute-start.8 = (s32[2,1024]{1,0:T(2,128)}, s32[2,1024]{1,0:T(2,128)}, u32[]{:S(2)}, u32[]{:S(2)}) collective-permute-start(s32[2,1024]{1,0:T(2,128)} %bitcast.247), channel_id=1, source_target_pairs={{0,4},{4,0},{8,12},{12,8},{16,20},{20,16},{24,28},{28,24},{1,5},{5... | collective-permute-start | bytes 24584 | tf_op jit(solution)/shard_map/ppermute | solution.py:38
  68.8 6.9 %reshape.446 = bf16[768,2304]{0,1:T(8,128)(2,1)S(1)} reshape(bf16[8,96,3,768]{1,0,3,2:T(8,128)(2,1)} %bitcast.284) | data formatting | bytes 7077888 | tf_op jit(solution)/shard_map/reshape | solution.py:184
  96.8 33.1 %reshape.449 = pred[12,512,1024]{2,1,0:T(32,128)(4,1)} reshape(pred[12,8,64,16,64]{4,3,2,1,0:T(8,128)(4,1)} %broadcast_in_dim.21) | data formatting | bytes 12582912 | tf_op jit(solution)/shard_map/reshape | solution.py:169
  151.6 14.2 %fusion.97 = (f32[12,512]{1,0:T(8,128)S(1)}, f32[12,512,1024]{2,1,0:T(8,128)}) fusion(bf16[512,12,64]{0,2,1:T(8,128)(2,1)S(1)} %bitcast.298, bf16[1024,12,64]{0,2,1:T(8,128)(2,1)S(1)} %bitcast.295, pred[12,512,1024]{2,1,0:T(32,128)(4,1)} %reshape.449, pred[512,1024]{1,0:T(8,128)(4,1)S(1)} %broadcast_compare_fusion), kind=kOutput, calls=%fused_computation.284 | convolution fusion | flops 830466048 | bytes 34365440 | tf_op jit(solution)/shard_map/qhd,khd->hqk/dot_general | solution.py:203
  165.8 11.6 %fusion = f32[12,512]{1,0:T(8,128)S(1)} fusion(f32[12,512,1024]{2,1,0:T(8,128)} %get-tuple-element.116, f32[12,512]{1,0:T(8,128)S(1)} %get-tuple-element.115), kind=kLoop, calls=%fused_computation.22 | loop fusion | flops 12576768 | bytes 25214976 | tf_op jit(solution)/shard_map/reduce_sum | solution.py:207
  177.5 10.4 %fusion.45 = bf16[12,64,512]{2,1,0:T(8,128)(2,1)S(1)} fusion(bf16[1024,12,64]{0,2,1:T(8,128)(2,1)S(1)} %bitcast.304, f32[12,512,1024]{2,1,0:T(8,128)} %get-tuple-element.116, f32[12,512]{1,0:T(8,128)S(1)} %fusion, f32[12,512]{1,0:T(8,128)S(1)} %get-tuple-element.115), kind=kOutput, calls=%fused_computation.121 | convolution fusion | flops 824573952 | bytes 27574272 | tf_op jit(solution)/shard_map/hqk,khd->qhd/dot_general | solution.py:210
  202.1 6.7 %fusion.92 = (bf16[8,384,768]{2,1,0:T(8,128)(2,1)}, bf16[8,384,768]{2,1,0:T(8,128)(2,1)S(1)}) fusion(bf16[8,864,768]{2,1,0:T(8,128)(2,1)} %dynamic-slice_dynamic-update-slice_fusion), kind=kLoop, calls=%fused_computation.279 | loop fusion | bytes 18874368 | tf_op jit(solution)/shard_map/slice | solution.py:192
  216.2 18.6 %multiply_convert_fusion.1 = (bf16[512,3072]{1,0:T(8,128)(2,1)S(1)}, f32[512,3072]{1,0:T(8,128)}, f32[512,3072]{1,0:T(8,128)}) fusion(f32[3072]{0:T(1024)S(1)} %add.341, bf16[768,3072]{1,0:T(8,128)(2,1)S(1)} %bitcast.306, f32[512,768]{1,0:T(8,128)S(1)} %get-tuple-element.118, f32[768]{0:T(1024)S(1)} %add.338, f32[768]{0:T(1024)S(1)} %mul.199, ...), kind=kOutput, calls=%fused_computation.38 | convolution fusion | flops 2521694208 | bytes 22042624 | tf_op jit(solution)/shard_map/dot_general | solution.py:215
  242.8 9.1 %convert_reduce_fusion = (f32[3072]{0:T(1024)S(1)}, bf16[512,3072]{1,0:T(8,128)(2,1)}) fusion(f32[512,3072]{1,0:T(8,128)} %get-tuple-element.65, f32[512,3072]{1,0:T(8,128)} %get-tuple-element.119, f32[3072]{0:T(1024)S(1)} %add.341, bf16[512,768]{1,0:T(8,128)(2,1)S(1)} %get-tuple-element.55, bf16[3072,768]{1,0:T(8,128)(2,1)S(1)} %bitcast.313), kind=kOutput, calls=%fused_computation.36 | convolution fusion | flops 2442654720 | bytes 21258240 | tf_op jit(solution)/shard_map/dot_general | solution.py:33
  260.3 19.9 %multiply_reduce_fusion = (f32[12,512]{1,0:T(8,128)S(1)}, f32[12,512,1024]{2,1,0:T(8,128)}) fusion(f32[12,512,1024]{2,1,0:T(8,128)} %get-tuple-element.116, f32[12,512]{1,0:T(8,128)S(1)} %log_add_fusion, bf16[512,12,64]{0,2,1:T(8,128)(2,1)S(1)} %bitcast.302, bf16[1024,12,64]{0,2,1:T(8,128)(2,1)S(1)} %bitcast.305), kind=kOutput, calls=%fused_computation.17 | convolution fusion | flops 824174592 | bytes 52740096 | tf_op jit(solution)/shard_map/qhd,khd->hqk/dot_general | solution.py:240
  280.2 11.9 %fusion.2 = f32[12,64,1024]{2,1,0:T(8,128)} fusion(bf16[512,12,64]{0,2,1:T(8,128)(2,1)S(1)} %bitcast.303, f32[12,512,1024]{2,1,0:T(8,128)} %get-tuple-element.116, f32[12,512]{1,0:T(8,128)S(1)} %log_add_fusion), kind=kOutput, calls=%fused_computation.24 | convolution fusion | flops 817889280 | bytes 29122560 | tf_op jit(solution)/shard_map/hqk,qhd->khd/dot_general | solution.py:246
  292.1 16.6 %multiply_convert_fusion = bf16[12,512,1024]{2,1,0:T(8,128)(2,1)S(1)} fusion(f32[12,512,1024]{2,1,0:T(8,128)} %get-tuple-element.124, f32[12,512,1024]{2,1,0:T(8,128)} %get-tuple-element.116, f32[12,512]{1,0:T(8,128)S(1)} %get-tuple-element.123, f32[12,512]{1,0:T(8,128)S(1)} %log_add_fusion), kind=kLoop, calls=%fused_computation.16 | loop fusion | flops 25165824 | bytes 62963712 | tf_op jit(solution)/shard_map/convert_element_type | solution.py:242
  319.0 9.1 %fusion.78 = f32[768,3072]{1,0:T(8,128)} fusion(bf16[512,3072]{1,0:T(8,128)(2,1)} %get-tuple-element.59, f32[512,768]{1,0:T(8,128)} %copy-done.9, f32[768]{0:T(1024)S(1)} %add.338, f32[768]{0:T(1024)S(1)} %mul.199, f32[512]{0:T(512)S(1)} %fusion.73, f32[512]{0:T(512)S(1)} %broadcast_multiply_fusion.1), kind=kOutput, calls=%fused_computation.270 | convolution fusion | flops 2417885184 | bytes 14166016 | tf_op jit(solution)/shard_map/dot_general | solution.py:29
  339.5 12.4 %reshape.470 = f32[8,96,4,768]{3,2,1,0:T(4,128)} reshape(f32[768,3072]{1,0:T(8,128)} %fusion.78) | data formatting | bytes 18874368 | tf_op jit(solution)/shard_map/reshape | solution.py:229
  385.6 10.4 %reshape.462 = f32[8,96,3,768]{1,0,3,2:T(8,128)} reshape(f32[768,2304]{0,1:T(8,128)} %fusion.54) | data formatting | bytes 14155776 | tf_op jit(solution)/shard_map/reshape | solution.py:229
  396.0 9.0 %copy.67 = f32[8,3,96,768]{3,2,1,0:T(8,128)} copy(f32[8,3,96,768]{2,0,3,1:T(8,128)} %bitcast.274) | data formatting | bytes 14155776 | tf_op jit(solution)/shard_map/transpose | solution.py:229
  424.6 11.4 %fusion.85 = (bf16[4,768,768]{2,1,0:T(8,128)(2,1)}, f32[4,768,768]{2,1,0:T(8,128)}) fusion(bf16[4,768,768]{2,1,0:T(8,128)(2,1)} %collective-permute-done.30, f32[4,2,768,768]{3,2,1,0:T(8,128)} %bitcast.294), kind=kLoop, calls=%fused_computation.275 | loop fusion | flops 7077888 | bytes 28311552 | tf_op jit(solution)/shard_map/convert.11
  442.3 10.7 %collective-permute-done.31 = bf16[384,768]{1,0:T(8,128)(2,1)S(1)} collective-permute-done((bf16[384,768]{1,0:T(8,128)(2,1)S(1)}, bf16[384,768]{1,0:T(8,128)(2,1)S(1)}, u32[]{:S(2)}, u32[]{:S(2)}) %collective-permute-start.31) | collective-permute-done | bytes 589856 | tf_op jit(solution)/shard_map/ppermute | solution.py:38
  473.6 26.8 %collective-permute-done.25 = bf16[400,768]{1,0:T(8,128)(2,1)} collective-permute-done((bf16[400,768]{1,0:T(8,128)(2,1)}, bf16[400,768]{1,0:T(8,128)(2,1)}, u32[]{:S(2)}, u32[]{:S(2)}) %collective-permute-start.25) | collective-permute-done | bytes 614432 | tf_op jit(solution)/shard_map/ppermute | solution.py:38
  512.0 15.7 %collective-permute-done.26 = bf16[192,768]{1,0:T(8,128)(2,1)S(1)} collective-permute-done((bf16[192,768]{1,0:T(8,128)(2,1)S(1)}, bf16[192,768]{1,0:T(8,128)(2,1)S(1)}, u32[]{:S(2)}, u32[]{:S(2)}) %collective-permute-start.26) | collective-permute-done | bytes 294944 | tf_op jit(solution)/shard_map/ppermute | solution.py:38
  534.6 12.4 %collective-permute-done.35 = bf16[384,768]{1,0:T(8,128)(2,1)S(1)} collective-permute-done((bf16[384,768]{1,0:T(8,128)(2,1)S(1)}, bf16[384,768]{1,0:T(8,128)(2,1)S(1)}, u32[]{:S(2)}, u32[]{:S(2)}) %collective-permute-start.35) | collective-permute-done | bytes 589856 | tf_op jit(solution)/shard_map/ppermute | solution.py:38
  553.7 13.1 %collective-permute-start.38 = (bf16[384,768]{1,0:T(8,128)(2,1)S(1)}, bf16[384,768]{1,0:T(8,128)(2,1)}, u32[]{:S(2)}, u32[]{:S(2)}) collective-permute-start(bf16[384,768]{1,0:T(8,128)(2,1)S(1)} %get-tuple-element.95), channel_id=1, source_target_pairs={{0,1},{1,0},{2,3},{3,2},{4,5},{5,4},{6,7},{7,6},{8,9},{9,8},{10,11... | collective-permute-start | bytes 1769480 | tf_op jit(solution)/shard_map/ppermute | solution.py:38
  574.3 7.2 %collective-permute-done.38 = bf16[384,768]{1,0:T(8,128)(2,1)} collective-permute-done((bf16[384,768]{1,0:T(8,128)(2,1)S(1)}, bf16[384,768]{1,0:T(8,128)(2,1)}, u32[]{:S(2)}, u32[]{:S(2)}) %collective-permute-start.38) | collective-permute-done | bytes 589856 | tf_op jit(solution)/shard_map/ppermute | solution.py:38
  (405 shorter events, 260.5 us)
Async XLA Ops:
  28.0 29.7 %collective-permute-start.6 = (bf16[4,304,768]{2,1,0:T(8,128)(2,1)}, bf16[4,304,768]{2,1,0:T(8,128)(2,1)}, u32[]{:S(2)}, u32[]{:S(2)}) collective-permute-start(bf16[4,304,768]{2,1,0:T(8,128)(2,1)} %get-tuple-element.89), channel_id=1, source_target_pairs={{0,4},{4,0},{8,12},{12,8},{16,20},{20,16},{24,28},{28,24},{1,5},{5... | collective-permute-start | bytes 5603336 | tf_op jit(solution)/shard_map/ppermute | solution.py:38
  29.7 56.0 %collective-permute-start.10 = (bf16[864,768]{1,0:T(8,128)(2,1)}, bf16[864,768]{1,0:T(8,128)(2,1)}, u32[]{:S(2)}, u32[]{:S(2)}) collective-permute-start(bf16[864,768]{1,0:T(8,128)(2,1)} %get-tuple-element.94), channel_id=1, source_target_pairs={{0,16},{4,20},{8,24},{12,28},{16,0},{20,4},{24,8},{28,12},{1,17},{... | collective-permute-start | bytes 3981320 | tf_op jit(solution)/shard_map/ppermute | solution.py:38
  31.3 57.7 %collective-permute-start.9 = (bf16[864,768]{1,0:T(8,128)(2,1)}, bf16[864,768]{1,0:T(8,128)(2,1)}, u32[]{:S(2)}, u32[]{:S(2)}) collective-permute-start(bf16[864,768]{1,0:T(8,128)(2,1)} %get-tuple-element.94), channel_id=1, source_target_pairs={{0,8},{4,12},{8,0},{12,4},{16,24},{20,28},{24,16},{28,20},{1,9},{5... | collective-permute-start | bytes 3981320 | tf_op jit(solution)/shard_map/ppermute | solution.py:38
  40.6 89.3 %collective-permute-start.8 = (s32[2,1024]{1,0:T(2,128)}, s32[2,1024]{1,0:T(2,128)}, u32[]{:S(2)}, u32[]{:S(2)}) collective-permute-start(s32[2,1024]{1,0:T(2,128)} %bitcast.247), channel_id=1, source_target_pairs={{0,4},{4,0},{8,12},{12,8},{16,20},{20,16},{24,28},{28,24},{1,5},{5... | collective-permute-start | bytes 24584 | tf_op jit(solution)/shard_map/ppermute | solution.py:38
  55.3 182.8 %collective-permute-start.17 = (bf16[256,768]{1,0:T(8,128)(2,1)}, bf16[256,768]{1,0:T(8,128)(2,1)}, u32[]{:S(2)}, u32[]{:S(2)}) collective-permute-start(bf16[256,768]{1,0:T(8,128)(2,1)} %get-tuple-element.102), channel_id=1, source_target_pairs={{0,2},{1,0},{2,6},{3,4},{4,3},{5,1},{6,7},{7,5},{8,10},{9,8},{10,1... | collective-permute-start | bytes 1179656 | tf_op jit(solution)/shard_map/ppermute | solution.py:107
  84.1 61.2 %collective-permute-start.7 = (bf16[2,512,768]{2,1,0:T(8,128)(2,1)}, bf16[2,512,768]{2,1,0:T(8,128)(2,1)}, u32[]{:S(2)}, u32[]{:S(2)}) collective-permute-start(bf16[2,512,768]{2,1,0:T(8,128)(2,1)} %pad_maximum_fusion.8), channel_id=1, source_target_pairs={{0,4},{4,0},{8,12},{12,8},{16,20},{20,16},{24,28},{28,24},{1,5},{5... | collective-permute-start | bytes 4718600 | tf_op jit(solution)/shard_map/ppermute | solution.py:38
  87.7 48.1 %collective-permute-start.12 = (bf16[432,768]{1,0:T(8,128)(2,1)}, bf16[432,768]{1,0:T(8,128)(2,1)}, u32[]{:S(2)}, u32[]{:S(2)}) collective-permute-start(bf16[432,768]{1,0:T(8,128)(2,1)} %slice.310), channel_id=1, source_target_pairs={{0,8},{4,12},{8,0},{12,4},{16,24},{20,28},{24,16},{28,20},{1,9},{5... | collective-permute-start | bytes 1990664 | tf_op jit(solution)/shard_map/ppermute | solution.py:38
  91.0 44.9 %collective-permute-start.11 = (bf16[432,768]{1,0:T(8,128)(2,1)}, bf16[432,768]{1,0:T(8,128)(2,1)}, u32[]{:S(2)}, u32[]{:S(2)}) collective-permute-start(bf16[432,768]{1,0:T(8,128)(2,1)} %slice.309), channel_id=1, source_target_pairs={{0,16},{4,20},{8,24},{12,28},{16,0},{20,4},{24,8},{28,12},{1,17},{... | collective-permute-start | bytes 1990664 | tf_op jit(solution)/shard_map/ppermute | solution.py:38
  129.9 108.2 %collective-permute-start.16 = (bf16[256,768]{1,0:T(8,128)(2,1)}, bf16[256,768]{1,0:T(8,128)(2,1)}, u32[]{:S(2)}, u32[]{:S(2)}) collective-permute-start(bf16[256,768]{1,0:T(8,128)(2,1)} %get-tuple-element.101), channel_id=1, source_target_pairs={{0,0},{1,2},{2,4},{3,6},{4,1},{5,3},{6,5},{7,7},{8,8},{9,10},{10,1... | collective-permute-start | bytes 1179656 | tf_op jit(solution)/shard_map/ppermute | solution.py:107
  142.6 45.3 %collective-permute-start.13 = (bf16[4,864,768]{2,1,0:T(8,128)(2,1)}, bf16[4,864,768]{2,1,0:T(8,128)(2,1)}, u32[]{:S(2)}, u32[]{:S(2)}) collective-permute-start(bf16[4,864,768]{2,1,0:T(8,128)(2,1)} %get-tuple-element.75), channel_id=1, source_target_pairs={{0,4},{4,0},{8,12},{12,8},{16,20},{20,16},{24,28},{28,24},{1,5},{5... | collective-permute-start | bytes 15925256 | tf_op jit(solution)/shard_map/ppermute | solution.py:38
  334.9 39.2 %collective-permute-start.18 = (bf16[2,512,768]{1,2,0:T(8,128)(2,1)}, bf16[2,512,768]{1,2,0:T(8,128)(2,1)}, u32[]{:S(2)}, u32[]{:S(2)}) collective-permute-start(bf16[2,512,768]{1,2,0:T(8,128)(2,1)} %fusion.18), channel_id=1, source_target_pairs={{0,4},{4,0},{8,12},{12,8},{16,20},{20,16},{24,28},{28,24},{1,5},{5... | collective-permute-start | bytes 4718600 | tf_op jit(solution)/shard_map/ppermute | solution.py:38
  373.2 51.4 %collective-permute-start.30 = (bf16[4,768,768]{2,1,0:T(8,128)(2,1)}, bf16[4,768,768]{2,1,0:T(8,128)(2,1)}, u32[]{:S(2)}, u32[]{:S(2)}) collective-permute-start(bf16[4,768,768]{2,1,0:T(8,128)(2,1)} %fusion.14), channel_id=1, source_target_pairs={{0,4},{4,0},{8,12},{12,8},{16,20},{20,16},{24,28},{28,24},{1,5},{5... | collective-permute-start | bytes 14155784 | tf_op jit(solution)/shard_map/ppermute | solution.py:38
  412.2 54.3 %collective-permute-start.15 = (bf16[256,768]{1,0:T(8,128)(2,1)}, bf16[256,768]{1,0:T(8,128)(2,1)}, u32[]{:S(2)}, u32[]{:S(2)}) collective-permute-start(bf16[256,768]{1,0:T(8,128)(2,1)} %get-tuple-element.104), channel_id=1, source_target_pairs={{2,0},{0,1},{6,2},{4,3},{3,4},{1,5},{7,6},{5,7},{10,8},{8,9},{14,1... | collective-permute-start | bytes 1179656 | tf_op jit(solution)/shard_map/ppermute | solution.py:116
  412.2 55.8 %collective-permute-start.14 = (bf16[256,768]{1,0:T(8,128)(2,1)}, bf16[256,768]{1,0:T(8,128)(2,1)}, u32[]{:S(2)}, u32[]{:S(2)}) collective-permute-start(bf16[256,768]{1,0:T(8,128)(2,1)} %get-tuple-element.103), channel_id=1, source_target_pairs={{0,0},{2,1},{4,2},{6,3},{1,4},{3,5},{5,6},{7,7},{8,8},{10,9},{12,1... | collective-permute-start | bytes 1179656 | tf_op jit(solution)/shard_map/ppermute | solution.py:116
  440.3 28.5 %collective-permute-start.20 = (bf16[256,768]{1,0:T(8,128)(2,1)}, bf16[256,768]{1,0:T(8,128)(2,1)}, u32[]{:S(2)}, u32[]{:S(2)}) collective-permute-start(bf16[256,768]{1,0:T(8,128)(2,1)} %get-tuple-element.100), channel_id=1, source_target_pairs={{2,0},{0,1},{6,2},{4,3},{3,4},{1,5},{7,6},{5,7},{10,8},{8,9},{14,1... | collective-permute-start | bytes 1179656 | tf_op jit(solution)/shard_map/ppermute | solution.py:116
  456.3 50.2 %collective-permute-start.34 = (bf16[768,768]{1,0:T(8,128)(2,1)S(1)}, bf16[768,768]{1,0:T(8,128)(2,1)S(1)}, u32[]{:S(2)}, u32[]{:S(2)}) collective-permute-start(bf16[768,768]{1,0:T(8,128)(2,1)S(1)} %pad_maximum_fusion.11), channel_id=1, source_target_pairs={{0,16},{4,20},{8,24},{12,28},{16,0},{20,4},{24,8},{28,12},{1,17},{... | collective-permute-start | bytes 3538952 | tf_op jit(solution)/shard_map/ppermute | solution.py:38
  463.5 43.0 %collective-permute-start.32 = (bf16[768,768]{1,0:T(8,128)(2,1)S(1)}, bf16[768,768]{1,0:T(8,128)(2,1)}, u32[]{:S(2)}, u32[]{:S(2)}) collective-permute-start(bf16[768,768]{1,0:T(8,128)(2,1)S(1)} %pad_maximum_fusion.10), channel_id=1, source_target_pairs={{0,8},{4,12},{8,0},{12,4},{16,24},{20,28},{24,16},{28,20},{1,9},{5... | collective-permute-start | bytes 3538952 | tf_op jit(solution)/shard_map/ppermute | solution.py:38
  466.5 33.9 %collective-permute-start.25 = (bf16[400,768]{1,0:T(8,128)(2,1)}, bf16[400,768]{1,0:T(8,128)(2,1)}, u32[]{:S(2)}, u32[]{:S(2)}) collective-permute-start(bf16[400,768]{1,0:T(8,128)(2,1)} %pad_maximum_fusion.19), channel_id=1, source_target_pairs={{0,16},{4,20},{8,24},{12,28},{16,0},{20,4},{24,8},{28,12},{1,17},{... | collective-permute-start | bytes 1843208 | tf_op jit(solution)/shard_map/ppermute | solution.py:38
  468.0 33.4 %collective-permute-start.23 = (bf16[400,768]{1,0:T(8,128)(2,1)}, bf16[400,768]{1,0:T(8,128)(2,1)}, u32[]{:S(2)}, u32[]{:S(2)}) collective-permute-start(bf16[400,768]{1,0:T(8,128)(2,1)} %pad_maximum_fusion.18), channel_id=1, source_target_pairs={{0,8},{4,12},{8,0},{12,4},{16,24},{20,28},{24,16},{28,20},{1,9},{5... | collective-permute-start | bytes 1843208 | tf_op jit(solution)/shard_map/ppermute | solution.py:38
  503.3 26.7 %collective-permute-start.28 = (bf16[208,768]{1,0:T(8,128)(2,1)S(1)}, bf16[208,768]{1,0:T(8,128)(2,1)S(1)}, u32[]{:S(2)}, u32[]{:S(2)}) collective-permute-start(bf16[208,768]{1,0:T(8,128)(2,1)S(1)} %slice.340), channel_id=1, source_target_pairs={{0,3},{1,2},{2,1},{3,0},{4,7},{5,6},{6,5},{7,4},{8,11},{9,10},{10,... | collective-permute-start | bytes 958472 | tf_op jit(solution)/shard_map/ppermute | solution.py:38
  510.0 37.0 %collective-permute-start.35 = (bf16[384,768]{1,0:T(8,128)(2,1)S(1)}, bf16[384,768]{1,0:T(8,128)(2,1)S(1)}, u32[]{:S(2)}, u32[]{:S(2)}) collective-permute-start(bf16[384,768]{1,0:T(8,128)(2,1)S(1)} %get-tuple-element.98), channel_id=1, source_target_pairs={{0,1},{1,0},{2,3},{3,2},{4,5},{5,4},{6,7},{7,6},{8,9},{9,8},{10,11... | collective-permute-start | bytes 1769480 | tf_op jit(solution)/shard_map/ppermute | solution.py:38
  527.8 25.8 %collective-permute-start.27 = (bf16[192,768]{1,0:T(8,128)(2,1)S(1)}, bf16[192,768]{1,0:T(8,128)(2,1)S(1)}, u32[]{:S(2)}, u32[]{:S(2)}) collective-permute-start(bf16[192,768]{1,0:T(8,128)(2,1)S(1)} %add_convert_fusion.8), channel_id=1, source_target_pairs={{0,3},{1,2},{2,1},{3,0},{4,7},{5,6},{6,5},{7,4},{8,11},{9,10},{10,... | collective-permute-start | bytes 884744 | tf_op jit(solution)/shard_map/ppermute | solution.py:38
  530.0 36.7 %collective-permute-start.29 = (bf16[208,768]{1,0:T(8,128)(2,1)S(1)}, bf16[208,768]{1,0:T(8,128)(2,1)S(1)}, u32[]{:S(2)}, u32[]{:S(2)}) collective-permute-start(bf16[208,768]{1,0:T(8,128)(2,1)S(1)} %add_convert_fusion.7), channel_id=1, source_target_pairs={{0,1},{1,0},{2,3},{3,2},{4,5},{5,4},{6,7},{7,6},{8,9},{9,8},{10,11... | collective-permute-start | bytes 958472 | tf_op jit(solution)/shard_map/ppermute | solution.py:38
  553.7 27.8 %collective-permute-start.38 = (bf16[384,768]{1,0:T(8,128)(2,1)S(1)}, bf16[384,768]{1,0:T(8,128)(2,1)}, u32[]{:S(2)}, u32[]{:S(2)}) collective-permute-start(bf16[384,768]{1,0:T(8,128)(2,1)S(1)} %get-tuple-element.95), channel_id=1, source_target_pairs={{0,1},{1,0},{2,3},{3,2},{4,5},{5,4},{6,7},{7,6},{8,9},{9,8},{10,11... | collective-permute-start | bytes 1769480 | tf_op jit(solution)/shard_map/ppermute | solution.py:38
  (79 other events, 742.7 us)
